TPU v7x, 32 devices: a whole 2x2x4 slice. The times are simulated.
32 devices in a mesh: trial: 4 (over z), row: 8 (over y, x, core).
Axes of the slice: x: 2, y: 2, z: 4, core: 2. Of those that a mesh axis runs over, the one named last changes fastest.
Arguments:
- phase_map: float32 [4096, 512], P('row'), may hold values from -3.140625 to 3.140625
- target: float32 [4096, 512], P('row'), may hold values from 0 to 2
- distance: float32 [4], P('trial'), may hold values from 0.25 to 1
- etch_class: int32 [4, 32, 4], P('trial', 'row'), may hold values from 0 to 3
- class_offset: float32 [4], replicated, may hold values from -0.6 to 0.6
- aperture_start: int32 [4], replicated, may hold values from 0 to 7
- aperture_stop: int32 [4], replicated, may hold values from 25 to 32
Outputs:
- phase_grad: float32 [4096, 512], P('row', 'trial')
Inputs may be any that keep to these rules, and one draw needn't show every extreme that they name: `etch_class`: etch bias classes.
All inputs are finite; a program needn't handle non-finite values.
Results may differ from a plain program's by a relative error of at most 0.02.
Values may be sent and summed in bfloat16 or wider, within the bound.
A program may use at most 64 MiB of HBM per device.

v0:
```python
import jax
import jax.numpy as jnp
from jax import lax
from jax.sharding import PartitionSpec as P

BLK = 128
HIGHEST_PRECISION = lax.Precision.HIGHEST


def cosine_pair(numer, denom):
    angle = -2.0 * jnp.pi / denom * numer.astype(jnp.float32)
    return (jnp.cos(angle), jnp.sin(angle))


def column_tables(width, kept):
    columns = jnp.arange(width, dtype=jnp.int32)
    freqs = jnp.arange(kept, dtype=jnp.int32) - kept // 2
    table_real, table_imag = cosine_pair(jnp.mod(columns[:, None] * freqs[None, :], width), width)
    table_real = table_real.astype(jnp.bfloat16)
    table_imag = table_imag.astype(jnp.bfloat16)
    forward = jnp.concatenate(
        [
            jnp.concatenate([table_real, table_imag], 1),
            jnp.concatenate([-table_imag, table_real], 1),
        ],
        0,
    )
    backward = jnp.concatenate(
        [
            jnp.concatenate([table_real.T, -table_imag.T], 1),
            jnp.concatenate([table_imag.T, table_real.T], 1),
        ],
        0,
    )
    return (forward, backward)


def block_tables(height):
    places = jnp.arange(height, dtype=jnp.int32)
    table_real, table_imag = cosine_pair(jnp.mod(places[:, None] * places[None, :], height), height)
    table_real = table_real.astype(jnp.bfloat16)
    table_imag = table_imag.astype(jnp.bfloat16)
    forward = jnp.concatenate(
        [
            jnp.concatenate([table_real, -table_imag], 1),
            jnp.concatenate([table_imag, table_real], 1),
        ],
        0,
    )
    backward = jnp.concatenate(
        [
            jnp.concatenate([table_real, table_imag], 1),
            jnp.concatenate([-table_imag, table_real], 1),
        ],
        0,
    )
    return (forward, backward)


def transfer_phase(signed, across, dist, global_rows, width):
    row_freq = signed.astype(jnp.float32)
    col_freq = across.astype(jnp.float32)
    theta = (
        -jnp.pi
        * dist
        * (
            row_freq * row_freq * (1.0 / global_rows)
            + col_freq * col_freq * (global_rows / (width * width))
        )
    )
    return (jnp.cos(theta), jnp.sin(theta))


def small_einsum(form, table, values):
    return jnp.einsum(form, table, values, precision=HIGHEST_PRECISION)


def local(phase_map, target, distance, etch_class, class_offset, aperture_start, aperture_stop):
    height, width = phase_map.shape
    kept = width // 2
    groups = lax.axis_size("row")
    device = lax.axis_index("row")
    global_rows = height * groups
    slim_cols = kept // groups
    col_fwd, col_back = column_tables(width, kept)
    blk_fwd, blk_back = block_tables(height)
    group_ids = jnp.arange(groups, dtype=jnp.int32)
    small_real, small_imag = cosine_pair(
        jnp.mod(group_ids[:, None] * group_ids[None, :], groups), groups
    )
    local_rows = jnp.arange(height, dtype=jnp.int32)
    dist = distance[0]
    classes = etch_class[0]
    row_blocks, col_blocks = classes.shape
    levels = jnp.arange(class_offset.shape[0], dtype=jnp.int32)
    offsets = jnp.sum(jnp.where(classes[:, :, None] == levels, class_offset, 0.0), axis=2)
    offset_map = jnp.broadcast_to(
        offsets[:, None, :, None], (row_blocks, BLK, col_blocks, BLK)
    ).reshape(height, width)
    row_block = (device * height + local_rows) // BLK
    first_block = jnp.broadcast_to(aperture_start[:, None], (col_blocks, BLK)).reshape(width)
    stop_block = jnp.broadcast_to(aperture_stop[:, None], (col_blocks, BLK)).reshape(width)
    inside = (row_block[:, None] >= first_block[None, :]) & (
        row_block[:, None] < stop_block[None, :]
    )
    aperture_mask = inside.astype(jnp.float32)
    angle_map = phase_map + offset_map
    lens_real = aperture_mask * jnp.cos(angle_map)
    lens_imag = aperture_mask * jnp.sin(angle_map)
    twist_cols_real, twist_cols_imag = cosine_pair(
        jnp.mod(group_ids[:, None] * local_rows[None, :], global_rows), global_rows
    )
    twist_cols_real = twist_cols_real[None]
    twist_cols_imag = twist_cols_imag[None]

    def forward_columns(cols_real, cols_imag):
        parts = (
            lax.all_to_all(cols_real, "row", split_axis=0, concat_axis=1, tiled=True),
            lax.all_to_all(cols_imag, "row", split_axis=0, concat_axis=1, tiled=True),
        )
        part_real = parts[0].reshape(slim_cols, groups, height).astype(jnp.float32)
        part_imag = parts[1].reshape(slim_cols, groups, height).astype(jnp.float32)
        mixed_real = small_einsum("kp,cpl->ckl", small_real, part_real) - small_einsum(
            "kp,cpl->ckl", small_imag, part_imag
        )
        mixed_imag = small_einsum("kp,cpl->ckl", small_real, part_imag) + small_einsum(
            "kp,cpl->ckl", small_imag, part_real
        )
        turned_real = (mixed_real * twist_cols_real - mixed_imag * twist_cols_imag).astype(
            jnp.bfloat16
        )
        turned_imag = (mixed_real * twist_cols_imag + mixed_imag * twist_cols_real).astype(
            jnp.bfloat16
        )
        stacked = jnp.concatenate([turned_real, turned_imag], 2)
        spectrum = jnp.einsum("ckl,ol->cko", stacked, blk_fwd, preferred_element_type=jnp.float32)
        return (spectrum[:, :, :height], spectrum[:, :, height:])

    def inverse_columns(filtered_real, filtered_imag):
        stacked = jnp.concatenate([filtered_real, filtered_imag], 2)
        unmixed = jnp.einsum("ckl,ol->cko", stacked, blk_back, preferred_element_type=jnp.float32)
        unmixed_real = unmixed[:, :, :height]
        unmixed_imag = unmixed[:, :, height:]
        returned_real = (
            (unmixed_real * twist_cols_real + unmixed_imag * twist_cols_imag)
            .astype(jnp.bfloat16)
            .astype(jnp.float32)
        )
        returned_imag = (
            (unmixed_imag * twist_cols_real - unmixed_real * twist_cols_imag)
            .astype(jnp.bfloat16)
            .astype(jnp.float32)
        )
        near_real = (
            small_einsum("kp,ckl->cpl", small_real, returned_real)
            + small_einsum("kp,ckl->cpl", small_imag, returned_imag)
        ) * (1.0 / global_rows)
        near_imag = (
            small_einsum("kp,ckl->cpl", small_real, returned_imag)
            - small_einsum("kp,ckl->cpl", small_imag, returned_real)
        ) * (1.0 / global_rows)
        near_real = near_real.astype(jnp.bfloat16).reshape(slim_cols, global_rows)
        near_imag = near_imag.astype(jnp.bfloat16).reshape(slim_cols, global_rows)
        owned = (
            lax.all_to_all(near_real, "row", split_axis=1, concat_axis=0, tiled=True),
            lax.all_to_all(near_imag, "row", split_axis=1, concat_axis=0, tiled=True),
        )
        return (owned[0], owned[1])

    freq_rows = group_ids[None, :, None] + groups * local_rows[None, None, :]
    across = (device * slim_cols + jnp.arange(slim_cols, dtype=jnp.int32) - kept // 2)[
        :, None, None
    ]
    signed = jnp.mod(freq_rows + global_rows // 2, global_rows) - global_rows // 2
    filter_real, filter_imag = transfer_phase(signed, across, dist, global_rows, width)

    def propagate(field_real, field_imag, phase_real, phase_imag):
        stacked_field = jnp.concatenate([field_real, field_imag], 1)
        flipped = jnp.einsum(
            "rc,cj->jr", stacked_field, col_fwd, preferred_element_type=jnp.float32
        ).astype(jnp.bfloat16)
        spec_real, spec_imag = forward_columns(flipped[:kept], flipped[kept:])
        filtered_real = (spec_real * phase_real - spec_imag * phase_imag).astype(jnp.bfloat16)
        filtered_imag = (spec_real * phase_imag + spec_imag * phase_real).astype(jnp.bfloat16)
        near_real, near_imag = inverse_columns(filtered_real, filtered_imag)
        result = jnp.einsum(
            "jr,jo->ro",
            jnp.concatenate([near_real, near_imag], 0),
            col_back,
            preferred_element_type=jnp.float32,
        ) * (1.0 / width)
        return (result[:, :width], result[:, width:])

    focal_real, focal_imag = propagate(
        lens_real.astype(jnp.bfloat16), lens_imag.astype(jnp.bfloat16), filter_real, filter_imag
    )
    residual = focal_real * focal_real + focal_imag * focal_imag - target
    back_real, back_imag = propagate(
        (residual * focal_real).astype(jnp.bfloat16),
        (residual * focal_imag).astype(jnp.bfloat16),
        filter_real,
        -filter_imag,
    )
    gradient = 2.0 * (lens_real * back_imag - lens_imag * back_real)
    return lax.psum_scatter(
        gradient.astype(jnp.bfloat16), "trial", scatter_dimension=1, tiled=True
    ).astype(jnp.float32)


def solution(mesh):
    return jax.shard_map(
        local,
        mesh=mesh,
        in_specs=(
            P("row", None),
            P("row", None),
            P("trial"),
            P("trial", "row", None),
            P(),
            P(),
            P(),
        ),
        out_specs=P("row", "trial"),
        check_vma=False,
    )
```

profile of v0, /device:TPU:0, one launch (start us, length us, event | category | flops | bytes accessed | tf_op | source)
XLA Modules:
  0.0 170.8 jit_solution(2126734685454798621)
XLA Ops:
  6.5 2.0 %fusion.99 = bf16[512,256]{1,0:T(8,128)(2,1)S(1)} fusion(s32[256]{0:T(256)S(1)} %iota_add_fusion.1), kind=kLoop, calls=%fused_computation.150 | loop fusion | flops 2359296 | bytes 263168 | tf_op jit(solution)/shard_map/neg | solution.py:24
  8.6 2.2 %sine_convert_fusion.2 = (bf16[512,256]{1,0:T(8,128)(2,1)S(1)}, bf16[512,256]{1,0:T(8,128)(2,1)S(1)}) fusion(s32[256]{0:T(256)S(1)} %iota_add_fusion.1), kind=kLoop, calls=%fused_computation.123 | loop fusion | flops 2097152 | bytes 525312 | tf_op jit(solution)/shard_map/convert_element_type | solution.py:20
  10.8 0.9 select_reduce_fusion
  12.7 4.2 %fusion.43 = (bf16[512,512]{1,0:T(8,128)(2,1)S(1)}, bf16[512,512]{1,0:T(8,128)(2,1)S(1)}) fusion(s32[512]{0:T(512)S(1)} %get-tuple-element.29, s32[512]{0:T(512)S(1)} %get-tuple-element.30, s32[512]{0:T(512)S(1)} %add_select_fusion.6, f32[512,512]{1,0:T(8,128)S(1)} %copy-done, f32[64,8,4,128]{3,2,1,0:T(4,128)S(1)} %bitcast.136), kind=kLoop, calls=%fused_computation.77 | loop fusion | flops 2097152 | bytes 3151872 | tf_op jit(solution)/shard_map/convert_element_type | solution.py:195
  17.7 0.8 fusion.234
  18.6 5.2 %all-to-all-start = ((bf16[8,32,512]{2,1,0:T(8,128)(2,1)}), bf16[8,32,512]{2,1,0:T(8,128)(2,1)S(1)}, u32[]{:S(2)}, u32[]{:S(2)}) async-start(bf16[8,32,512]{2,1,0:T(8,128)(2,1)} %bitcast.3), calls=%async_computation | async-start | bytes 524288 | tf_op jit(solution)/shard_map/all_to_all | solution.py:118
  23.9 4.6 %fusion.98 = bf16[512,512]{1,0:T(8,128)(2,1)} fusion(), kind=kLoop, calls=%fused_computation.149 | loop fusion | flops 4718592 | bytes 524288 | tf_op jit(solution)/shard_map/neg | solution.py:45
  28.5 4.6 %cosine_convert_fusion = bf16[512,512]{1,0:T(8,128)(2,1)} fusion(), kind=kLoop, calls=%fused_computation.64 | loop fusion | flops 3932160 | bytes 524288 | tf_op jit(solution)/shard_map/convert_element_type | solution.py:41
  33.1 4.6 %sine_convert_fusion = bf16[512,512]{1,0:T(8,128)(2,1)} fusion(), kind=kLoop, calls=%fused_computation.63 | loop fusion | flops 3932160 | bytes 524288 | tf_op jit(solution)/shard_map/convert_element_type | solution.py:42
  37.7 3.1 %sine_convert_fusion.1 = (bf16[256,512]{1,0:T(8,128)(2,1)S(1)}, bf16[256,512]{1,0:T(8,128)(2,1)}) fusion(s32[256]{0:T(256)S(1)} %iota_add_fusion.1), kind=kLoop, calls=%fused_computation.109 | loop fusion | flops 2097152 | bytes 525312 | tf_op jit(solution)/shard_map/convert_element_type | solution.py:20
  41.5 4.2 %all-to-all-start.1 = ((bf16[8,32,512]{2,1,0:T(8,128)(2,1)}), bf16[8,32,512]{2,1,0:T(8,128)(2,1)S(1)}, u32[]{:S(2)}, u32[]{:S(2)}) async-start(bf16[8,32,512]{2,1,0:T(8,128)(2,1)} %bitcast.6), calls=%async_computation.1 | async-start | bytes 524288 | tf_op jit(solution)/shard_map/all_to_all | solution.py:119
  46.2 6.4 %all-to-all-done.1 = bf16[8,32,512]{2,1,0:T(8,128)(2,1)S(1)} async-done(((bf16[8,32,512]{2,1,0:T(8,128)(2,1)}), bf16[8,32,512]{2,1,0:T(8,128)(2,1)S(1)}, u32[]{:S(2)}, u32[]{:S(2)}) %all-to-all-start.1) | async-done | bytes 262176 | tf_op jit(solution)/shard_map/all_to_all | solution.py:119
  55.0 2.3 %subtract_convert_fusion.4 = (bf16[32,8,512]{2,1,0:T(8,128)(2,1)S(1)}, bf16[32,8,512]{2,1,0:T(8,128)(2,1)S(1)}) fusion(f32[32,8,1024]{2,1,0:T(8,128)S(1)} %fusion.10, f32[32]{0:T(128)S(1)} %multiply_multiply_fusion, f32[8,512]{1,0:T(8,128)S(1)} %fusion.108, f32[]{:T(128)} %bitcast.14), kind=kLoop, calls=%fused_computation.116 | loop fusion | flops 1310720 | bytes 1589380 | tf_op jit(solution)/shard_map/convert_element_type | solution.py:183
  59.6 0.8 copy.58
  60.4 4.1 %all-to-all-start.2 = ((bf16[32,8,512]{2,0,1:T(8,128)(2,1)}), bf16[32,8,512]{2,0,1:T(8,128)(2,1)}, u32[]{:S(2)}, u32[]{:S(2)}) async-start(bf16[32,8,512]{2,0,1:T(8,128)(2,1)} %copy.58), calls=%async_computation.2 | async-start | bytes 524288 | tf_op jit(solution)/shard_map/all_to_all | solution.py:165
  65.6 5.7 %all-to-all-done.2 = bf16[32,8,512]{2,0,1:T(8,128)(2,1)} async-done(((bf16[32,8,512]{2,0,1:T(8,128)(2,1)}), bf16[32,8,512]{2,0,1:T(8,128)(2,1)}, u32[]{:S(2)}, u32[]{:S(2)}) %all-to-all-start.2) | async-done | bytes 262176 | tf_op jit(solution)/shard_map/all_to_all | solution.py:165
  71.4 3.4 %all-to-all-start.3 = ((bf16[32,8,512]{2,0,1:T(8,128)(2,1)}), bf16[32,8,512]{2,0,1:T(8,128)(2,1)S(1)}, u32[]{:S(2)}, u32[]{:S(2)}) async-start(bf16[32,8,512]{2,0,1:T(8,128)(2,1)} %copy.59), calls=%async_computation.3 | async-start | bytes 524288 | tf_op jit(solution)/shard_map/all_to_all | solution.py:166
  74.8 2.2 %fusion.100 = bf16[256,512]{1,0:T(8,128)(2,1)S(1)} fusion(s32[256]{0:T(256)S(1)} %iota_add_fusion.1), kind=kLoop, calls=%fused_computation.151 | loop fusion | flops 2359296 | bytes 263168 | tf_op jit(solution)/shard_map/neg | solution.py:30
  77.0 4.7 %all-to-all-done.3 = bf16[32,8,512]{2,0,1:T(8,128)(2,1)S(1)} async-done(((bf16[32,8,512]{2,0,1:T(8,128)(2,1)}), bf16[32,8,512]{2,0,1:T(8,128)(2,1)S(1)}, u32[]{:S(2)}, u32[]{:S(2)}) %all-to-all-start.3) | async-done | bytes 262176 | tf_op jit(solution)/shard_map/all_to_all | solution.py:166
  81.6 1.8 %convolution_multiply_fusion.1 = f32[512,1024]{1,0:T(8,128)S(1)} fusion(bf16[256,512]{1,0:T(8,128)(2,1)S(1)} %bitcast.140, bf16[256,512]{1,0:T(8,128)(2,1)} %bitcast.20, bf16[256,512]{1,0:T(8,128)(2,1)S(1)} %copy-done.8, bf16[256,512]{1,0:T(8,128)(2,1)S(1)} %get-tuple-element.25, bf16[256,512]{1,0:T(8,128)(2,1)S(1)} %fusion.100), kind=kOutput, calls=%fused_computation.9 | convolution fusion | flops 542638080 | bytes 3407872 | tf_op jit(solution)/shard_map/jr,jo->ro/dot_general | solution.py:186
  86.0 9.3 %all_to_all.128 = bf16[8,32,512]{2,1,0:T(8,128)(2,1)S(1)} all-to-all(bf16[8,32,512]{2,1,0:T(8,128)(2,1)S(1)} %bitcast.139), channel_id=1, replica_groups=mesh['trial'=4,'row'=8] {'row'}, dimensions={0} | all-to-all | bytes 524288 | tf_op jit(solution)/shard_map/all_to_all | solution.py:118
  95.3 3.6 %all-to-all-start.5 = ((bf16[8,32,512]{2,1,0:T(8,128)(2,1)}), bf16[8,32,512]{2,1,0:T(8,128)(2,1)S(1)}, u32[]{:S(2)}, u32[]{:S(2)}) async-start(bf16[8,32,512]{2,1,0:T(8,128)(2,1)} %bitcast.27), calls=%async_computation.5 | async-start | bytes 524288 | tf_op jit(solution)/shard_map/all_to_all | solution.py:119
  99.5 6.1 %all-to-all-done.5 = bf16[8,32,512]{2,1,0:T(8,128)(2,1)S(1)} async-done(((bf16[8,32,512]{2,1,0:T(8,128)(2,1)}), bf16[8,32,512]{2,1,0:T(8,128)(2,1)S(1)}, u32[]{:S(2)}, u32[]{:S(2)}) %all-to-all-start.5) | async-done | bytes 262176 | tf_op jit(solution)/shard_map/all_to_all | solution.py:119
  108.1 2.4 %subtract_convert_fusion.1 = (bf16[32,8,512]{2,1,0:T(8,128)(2,1)S(1)}, bf16[32,8,512]{2,1,0:T(8,128)(2,1)S(1)}) fusion(f32[32,8,1024]{2,1,0:T(8,128)S(1)} %fusion.8, f32[32]{0:T(128)S(1)} %multiply_multiply_fusion, f32[8,512]{1,0:T(8,128)S(1)} %fusion.108, f32[]{:T(128)} %bitcast.14), kind=kLoop, calls=%fused_computation.106 | loop fusion | flops 1441792 | bytes 1589380 | tf_op jit(solution)/shard_map/convert_element_type | solution.py:183
  113.4 4.0 %all-to-all-start.6 = ((bf16[32,8,512]{2,0,1:T(8,128)(2,1)}), bf16[32,8,512]{2,0,1:T(8,128)(2,1)}, u32[]{:S(2)}, u32[]{:S(2)}) async-start(bf16[32,8,512]{2,0,1:T(8,128)(2,1)} %copy.66), calls=%async_computation.6 | async-start | bytes 524288 | tf_op jit(solution)/shard_map/all_to_all | solution.py:165
  118.0 6.3 %all-to-all-done.6 = bf16[32,8,512]{2,0,1:T(8,128)(2,1)} async-done(((bf16[32,8,512]{2,0,1:T(8,128)(2,1)}), bf16[32,8,512]{2,0,1:T(8,128)(2,1)}, u32[]{:S(2)}, u32[]{:S(2)}) %all-to-all-start.6) | async-done | bytes 262176 | tf_op jit(solution)/shard_map/all_to_all | solution.py:165
  124.4 9.3 %all_to_all.129 = bf16[32,8,512]{2,0,1:T(8,128)(2,1)S(1)} all-to-all(bf16[32,8,512]{2,0,1:T(8,128)(2,1)S(1)} %copy.67), channel_id=1, replica_groups=mesh['trial'=4,'row'=8] {'row'}, dimensions={1} | all-to-all | bytes 524288 | tf_op jit(solution)/shard_map/all_to_all | solution.py:166
  133.7 1.8 %convolution_multiply_fusion = f32[512,1024]{1,0:T(8,128)S(1)} fusion(bf16[256,512]{1,0:T(8,128)(2,1)S(1)} %bitcast.141, bf16[256,512]{1,0:T(8,128)(2,1)} %bitcast.36, bf16[256,512]{1,0:T(8,128)(2,1)S(1)} %copy-done.9, bf16[256,512]{1,0:T(8,128)(2,1)S(1)} %get-tuple-element.25, bf16[256,512]{1,0:T(8,128)(2,1)} %copy-done.16), kind=kOutput, calls=%fused_computation.8 | convolution fusion | flops 542638080 | bytes 3407872 | tf_op jit(solution)/shard_map/jr,jo->ro/dot_general | solution.py:186
  135.5 4.3 %fusion.33 = bf16[512,512]{1,0:T(8,128)(2,1)S(1)} fusion(f32[512,1024]{1,0:T(8,128)S(1)} %convolution_multiply_fusion, s32[512]{0:T(512)S(1)} %get-tuple-element.29, s32[512]{0:T(512)S(1)} %get-tuple-element.30, s32[512]{0:T(512)S(1)} %add_select_fusion.6, f32[512,512]{1,0:T(8,128)S(1)} %copy-done, f32[64,8,4,128]{3,2,1,0:T(4,128)S(1)} %bitcast.137), kind=kLoop, calls=%fused_computation.50 | loop fusion | flops 2883584 | bytes 4724736 | tf_op jit(solution)/shard_map/convert_element_type | solution.py:206
  139.8 1.0 copy.84
  140.9 21.4 %reduce-scatter.4.cloned.1.call-done = bf16[128,512]{1,0:T(8,128)(2,1)} async-done(((bf16[512,512]{1,0:T(8,128)(2,1)}), bf16[128,512]{1,0:T(8,128)(2,1)}) %reduce-scatter.4.cloned.1.call-update) | async-done | bytes 131088
  162.2 1.0 copy.85
  (75 shorter events, 17.9 us)
Async XLA Ops:
  6.5 6.2 %copy-start = (f32[512,512]{1,0:T(8,128)S(1)}, f32[512,512]{1,0:T(8,128)}, u32[]{:S(2)}) copy-start(f32[512,512]{1,0:T(8,128)} %param.7) | copy-start | bytes 3145732
  8.6 8.4 %copy-start.10 = (bf16[512,256]{1,0:T(8,128)(2,1)}, bf16[512,256]{1,0:T(8,128)(2,1)S(1)}, u32[]{:S(2)}) copy-start(bf16[512,256]{1,0:T(8,128)(2,1)S(1)} %fusion.99) | copy-start | bytes 786436
  10.8 6.2 %copy-start.12 = (bf16[512,256]{1,0:T(8,128)(2,1)}, bf16[512,256]{1,0:T(8,128)(2,1)S(1)}, u32[]{:S(2)}) copy-start(bf16[512,256]{1,0:T(8,128)(2,1)S(1)} %get-tuple-element.27) | copy-start | bytes 786436
  10.8 6.2 %copy-start.14 = (bf16[512,256]{1,0:T(8,128)(2,1)}, bf16[512,256]{1,0:T(8,128)(2,1)S(1)}, u32[]{:S(2)}) copy-start(bf16[512,256]{1,0:T(8,128)(2,1)S(1)} %get-tuple-element.28) | copy-start | bytes 786436
  18.6 22.9 %all-to-all-start = ((bf16[8,32,512]{2,1,0:T(8,128)(2,1)}), bf16[8,32,512]{2,1,0:T(8,128)(2,1)S(1)}, u32[]{:S(2)}, u32[]{:S(2)}) async-start(bf16[8,32,512]{2,1,0:T(8,128)(2,1)} %bitcast.3), calls=%async_computation | async-start | bytes 524288 | tf_op jit(solution)/shard_map/all_to_all | solution.py:118
  41.5 11.1 %all-to-all-start.1 = ((bf16[8,32,512]{2,1,0:T(8,128)(2,1)}), bf16[8,32,512]{2,1,0:T(8,128)(2,1)S(1)}, u32[]{:S(2)}, u32[]{:S(2)}) async-start(bf16[8,32,512]{2,1,0:T(8,128)(2,1)} %bitcast.6), calls=%async_computation.1 | async-start | bytes 524288 | tf_op jit(solution)/shard_map/all_to_all | solution.py:119
  52.6 1.7 copy-start.2
  52.6 1.7 copy-start.4
  52.6 1.7 copy-start.6
  59.1 22.5 %copy-start.8 = (bf16[256,512]{1,0:T(8,128)(2,1)S(1)}, bf16[256,512]{1,0:T(8,128)(2,1)}, u32[]{:S(2)}) copy-start(bf16[256,512]{1,0:T(8,128)(2,1)} %get-tuple-element.26) | copy-start | bytes 786436
  60.4 11.0 %all-to-all-start.2 = ((bf16[32,8,512]{2,0,1:T(8,128)(2,1)}), bf16[32,8,512]{2,0,1:T(8,128)(2,1)}, u32[]{:S(2)}, u32[]{:S(2)}) async-start(bf16[32,8,512]{2,0,1:T(8,128)(2,1)} %copy.58), calls=%async_computation.2 | async-start | bytes 524288 | tf_op jit(solution)/shard_map/all_to_all | solution.py:165
  71.4 10.3 %all-to-all-start.3 = ((bf16[32,8,512]{2,0,1:T(8,128)(2,1)}), bf16[32,8,512]{2,0,1:T(8,128)(2,1)S(1)}, u32[]{:S(2)}, u32[]{:S(2)}) async-start(bf16[32,8,512]{2,0,1:T(8,128)(2,1)} %copy.59), calls=%async_computation.3 | async-start | bytes 524288 | tf_op jit(solution)/shard_map/all_to_all | solution.py:166
  76.9 8.3 %copy-start.16 = (bf16[256,512]{1,0:T(8,128)(2,1)}, bf16[256,512]{1,0:T(8,128)(2,1)S(1)}, u32[]{:S(2)}) copy-start(bf16[256,512]{1,0:T(8,128)(2,1)S(1)} %fusion.100) | copy-start | bytes 786436
  81.6 1.8 %copy-start.1 = (f32[512,512]{1,0:T(8,128)S(1)}, f32[512,512]{1,0:T(8,128)}, u32[]{:S(2)}) copy-start(f32[512,512]{1,0:T(8,128)} %param.8) | copy-start | bytes 3145732
  83.4 1.0 copy-start.11
  83.4 1.0 copy-start.13
  83.4 1.1 copy-start.15
  95.3 10.3 %all-to-all-start.5 = ((bf16[8,32,512]{2,1,0:T(8,128)(2,1)}), bf16[8,32,512]{2,1,0:T(8,128)(2,1)S(1)}, u32[]{:S(2)}, u32[]{:S(2)}) async-start(bf16[8,32,512]{2,1,0:T(8,128)(2,1)} %bitcast.27), calls=%async_computation.5 | async-start | bytes 524288 | tf_op jit(solution)/shard_map/all_to_all | solution.py:119
  105.6 1.7 copy-start.3
  105.6 1.7 copy-start.5
  105.6 1.7 copy-start.7
  112.2 21.5 %copy-start.9 = (bf16[256,512]{1,0:T(8,128)(2,1)S(1)}, bf16[256,512]{1,0:T(8,128)(2,1)}, u32[]{:S(2)}) copy-start(bf16[256,512]{1,0:T(8,128)(2,1)} %get-tuple-element.26) | copy-start | bytes 786436
  113.4 11.0 %all-to-all-start.6 = ((bf16[32,8,512]{2,0,1:T(8,128)(2,1)}), bf16[32,8,512]{2,0,1:T(8,128)(2,1)}, u32[]{:S(2)}, u32[]{:S(2)}) async-start(bf16[32,8,512]{2,0,1:T(8,128)(2,1)} %copy.66), calls=%async_computation.6 | async-start | bytes 524288 | tf_op jit(solution)/shard_map/all_to_all | solution.py:165
  117.5 44.7 %reduce-scatter.4.cloned.1.call-start = ((), (), s32[]{:S(2)}) async-start(), calls=%async_computation.9 | async-start | bytes 655360
Sparse Core Ops, SparseCore 0:
  141.0 21.1 reduce-scatter.3
where the time goes:
time: 172 us; the launch traced here: 171 us
  waiting for transfers between devices  50.6 us (29%)
  other arithmetic  39.1 us (23%)
  starting transfers between devices  24.6 us (14%)
  blocking collectives  18.6 us (11%)
  matrix products  15.7 us (9%)
  between operations  14.6 us (8%)
  local copies, waits for them, and re-layouts  7.68 us (4%)
    unnamed x2, waiting for transfers between devices  21.4 us
    all_to_all x2, waiting for transfers between devices, forward_columns(): lax.all_to_all(cols_imag, 'row', split_axis=0, concat_axis=1, tiled=True)  12.5 us
    all_to_all x2, waiting for transfers between devices, inverse_columns(): lax.all_to_all(near_real, 'row', split_axis=1, concat_axis=0, tiled=True)  12.1 us
    all_to_all x1, blocking collectives, inverse_columns(): lax.all_to_all(near_imag, 'row', split_axis=1, concat_axis=0, tiled=True)  9.3 us
    all_to_all x1, blocking collectives, forward_columns(): lax.all_to_all(cols_real, 'row', split_axis=0, concat_axis=1, tiled=True)  9.3 us
    all_to_all x2, starting transfers between devices, inverse_columns(): lax.all_to_all(near_real, 'row', split_axis=1, concat_axis=0, tiled=True)  8.1 us
    all_to_all x2, starting transfers between devices, forward_columns(): lax.all_to_all(cols_imag, 'row', split_axis=0, concat_axis=1, tiled=True)  7.84 us
    dot_general x16, matrix products, small_einsum(): return jnp.einsum(form, table, values, precision=HIGHEST_PRECISION)  7.7 us
  transfers between devices with their start and end apart: 7, of which 6 were waited for; matrix products, arithmetic and copies ran while one was open for 13% of the time, Pallas kernels for 0%

commit v1 on v0

--- a/solution.py
+++ b/solution.py
@@ -163,7 +163,12 @@
         near_imag = near_imag.astype(jnp.bfloat16).reshape(slim_cols, global_rows)
         owned = (
             lax.all_to_all(near_real, "row", split_axis=1, concat_axis=0, tiled=True),
-            lax.all_to_all(near_imag, "row", split_axis=1, concat_axis=0, tiled=True),
+            jnp.concatenate(
+                lax.all_to_all(
+                    jnp.stack(jnp.split(near_imag, lax.axis_size("row"), axis=1)), "row", 0, 0
+                ),
+                axis=0,
+            ),
         )
         return (owned[0], owned[1])
 

time: 172 us -> 172 us (level)
  waiting for transfers between devices: 50.6 us -> 46.2 us
  local copies, waits for them, and re-layouts: 7.68 us -> 12 us
    unnamed x36 -> x52, local copies, waits for them, and re-layouts: 2.73 us -> 7.25 us
    all_to_all x2, waiting for transfers between devices: 12.1 us -> 7.7 us  [inverse_columns(): lax.all_to_all(near_real, 'row', split_axis=1, concat_axis=0, tiled=True)]
  transfers between devices with their start and end apart: 7 -> 7, of which waited for: 6 -> 6; matrix products, arithmetic and copies ran while one was open for 13% -> 15% of each run, Pallas kernels for 0% -> 0%
where the time goes in v1:
time: 172 us; the launch traced here: 171 us
  waiting for transfers between devices  46.2 us (27%)
  other arithmetic  39.1 us (23%)
  starting transfers between devices  24.6 us (14%)
  blocking collectives  18.6 us (11%)
  matrix products  15.7 us (9%)
  between operations  14.6 us (8%)
  local copies, waits for them, and re-layouts  12 us (7%)
    unnamed x2, waiting for transfers between devices  21.4 us
    all_to_all x2, waiting for transfers between devices, forward_columns(): lax.all_to_all(cols_imag, 'row', split_axis=0, concat_axis=1, tiled=True)  12.5 us
    all_to_all x1, blocking collectives, inverse_columns(): lax.all_to_all(jnp.stack(jnp.split(near_imag, lax.axis_size('row'), axis=...  9.3 us
    all_to_all x1, blocking collectives, forward_columns(): lax.all_to_all(cols_real, 'row', split_axis=0, concat_axis=1, tiled=True)  9.3 us
    all_to_all x2, starting transfers between devices, inverse_columns(): lax.all_to_all(near_real, 'row', split_axis=1, concat_axis=0, tiled=True)  8.1 us
    all_to_all x2, starting transfers between devices, forward_columns(): lax.all_to_all(cols_imag, 'row', split_axis=0, concat_axis=1, tiled=True)  7.84 us
    dot_general x16, matrix products, small_einsum(): return jnp.einsum(form, table, values, precision=HIGHEST_PRECISION)  7.7 us
    all_to_all x2, waiting for transfers between devices, inverse_columns(): lax.all_to_all(near_real, 'row', split_axis=1, concat_axis=0, tiled=True)  7.7 us
  transfers between devices with their start and end apart: 7, of which 6 were waited for; matrix products, arithmetic and copies ran while one was open for 15% of the time, Pallas kernels for 0%

profile of v1, /device:TPU:0, one launch (start us, length us, event | category | flops | bytes accessed | tf_op | source)
XLA Modules:
  0.0 170.8 jit_solution(8615563389585557649)
XLA Ops:
  6.5 2.0 %fusion.97 = bf16[512,256]{1,0:T(8,128)(2,1)S(1)} fusion(s32[256]{0:T(256)S(1)} %iota_add_fusion.1), kind=kLoop, calls=%fused_computation.148 | loop fusion | flops 2359296 | bytes 263168 | tf_op jit(solution)/shard_map/neg | solution.py:24
  8.6 2.2 %sine_convert_fusion.2 = (bf16[512,256]{1,0:T(8,128)(2,1)S(1)}, bf16[512,256]{1,0:T(8,128)(2,1)S(1)}) fusion(s32[256]{0:T(256)S(1)} %iota_add_fusion.1), kind=kLoop, calls=%fused_computation.121 | loop fusion | flops 2097152 | bytes 525312 | tf_op jit(solution)/shard_map/convert_element_type | solution.py:20
  10.8 0.9 select_reduce_fusion
  12.7 4.2 %fusion.41 = (bf16[512,512]{1,0:T(8,128)(2,1)S(1)}, bf16[512,512]{1,0:T(8,128)(2,1)S(1)}) fusion(s32[512]{0:T(512)S(1)} %get-tuple-element.29, s32[512]{0:T(512)S(1)} %get-tuple-element.30, s32[512]{0:T(512)S(1)} %add_select_fusion.6, f32[512,512]{1,0:T(8,128)S(1)} %copy-done, f32[64,8,4,128]{3,2,1,0:T(4,128)S(1)} %bitcast.198), kind=kLoop, calls=%fused_computation.75 | loop fusion | flops 2097152 | bytes 3151872 | tf_op jit(solution)/shard_map/convert_element_type | solution.py:200
  17.7 0.8 fusion.232
  18.6 5.2 %all-to-all-start = ((bf16[8,32,512]{2,1,0:T(8,128)(2,1)}), bf16[8,32,512]{2,1,0:T(8,128)(2,1)S(1)}, u32[]{:S(2)}, u32[]{:S(2)}) async-start(bf16[8,32,512]{2,1,0:T(8,128)(2,1)} %bitcast.3), calls=%async_computation | async-start | bytes 524288 | tf_op jit(solution)/shard_map/all_to_all | solution.py:118
  23.9 4.6 %fusion.96 = bf16[512,512]{1,0:T(8,128)(2,1)} fusion(), kind=kLoop, calls=%fused_computation.147 | loop fusion | flops 4718592 | bytes 524288 | tf_op jit(solution)/shard_map/neg | solution.py:45
  28.5 4.6 %cosine_convert_fusion = bf16[512,512]{1,0:T(8,128)(2,1)} fusion(), kind=kLoop, calls=%fused_computation.62 | loop fusion | flops 3932160 | bytes 524288 | tf_op jit(solution)/shard_map/convert_element_type | solution.py:41
  33.1 4.6 %sine_convert_fusion = bf16[512,512]{1,0:T(8,128)(2,1)} fusion(), kind=kLoop, calls=%fused_computation.61 | loop fusion | flops 3932160 | bytes 524288 | tf_op jit(solution)/shard_map/convert_element_type | solution.py:42
  37.7 3.1 %sine_convert_fusion.1 = (bf16[256,512]{1,0:T(8,128)(2,1)S(1)}, bf16[256,512]{1,0:T(8,128)(2,1)}) fusion(s32[256]{0:T(256)S(1)} %iota_add_fusion.1), kind=kLoop, calls=%fused_computation.107 | loop fusion | flops 2097152 | bytes 525312 | tf_op jit(solution)/shard_map/convert_element_type | solution.py:20
  41.5 4.2 %all-to-all-start.1 = ((bf16[8,32,512]{2,1,0:T(8,128)(2,1)}), bf16[8,32,512]{2,1,0:T(8,128)(2,1)S(1)}, u32[]{:S(2)}, u32[]{:S(2)}) async-start(bf16[8,32,512]{2,1,0:T(8,128)(2,1)} %bitcast.6), calls=%async_computation.1 | async-start | bytes 524288 | tf_op jit(solution)/shard_map/all_to_all | solution.py:119
  46.2 6.4 %all-to-all-done.1 = bf16[8,32,512]{2,1,0:T(8,128)(2,1)S(1)} async-done(((bf16[8,32,512]{2,1,0:T(8,128)(2,1)}), bf16[8,32,512]{2,1,0:T(8,128)(2,1)S(1)}, u32[]{:S(2)}, u32[]{:S(2)}) %all-to-all-start.1) | async-done | bytes 262176 | tf_op jit(solution)/shard_map/all_to_all | solution.py:119
  55.0 2.3 %subtract_convert_fusion.4 = (bf16[32,8,512]{2,1,0:T(8,128)(2,1)S(1)}, bf16[32,8,512]{2,1,0:T(8,128)(2,1)S(1)}) fusion(f32[32,8,1024]{2,1,0:T(8,128)S(1)} %fusion.10, f32[32]{0:T(128)S(1)} %multiply_multiply_fusion, f32[8,512]{1,0:T(8,128)S(1)} %fusion.106, f32[]{:T(128)} %bitcast.14), kind=kLoop, calls=%fused_computation.114 | loop fusion | flops 1310720 | bytes 1589380 | tf_op jit(solution)/shard_map/convert_element_type | solution.py:188
  59.6 0.8 copy.54
  60.4 4.1 %all-to-all-start.2 = ((bf16[32,8,512]{2,0,1:T(8,128)(2,1)}), bf16[32,8,512]{2,0,1:T(8,128)(2,1)}, u32[]{:S(2)}, u32[]{:S(2)}) async-start(bf16[32,8,512]{2,0,1:T(8,128)(2,1)} %copy.54), calls=%async_computation.2 | async-start | bytes 524288 | tf_op jit(solution)/shard_map/all_to_all | solution.py:165
  69.9 1.5 all-to-all-done.2
  71.4 3.4 %all-to-all-start.3 = ((bf16[8,32,512]{2,1,0:T(8,128)(2,1)}), bf16[8,32,512]{2,1,0:T(8,128)(2,1)S(1)}, u32[]{:S(2)}, u32[]{:S(2)}) async-start(bf16[8,32,512]{2,1,0:T(8,128)(2,1)} %constant_dynamic-update-slice_fusion), calls=%async_computation.3 | async-start | bytes 524288 | tf_op jit(solution)/shard_map/all_to_all | solution.py:167
  74.8 2.2 %fusion.98 = bf16[256,512]{1,0:T(8,128)(2,1)S(1)} fusion(s32[256]{0:T(256)S(1)} %iota_add_fusion.1), kind=kLoop, calls=%fused_computation.149 | loop fusion | flops 2359296 | bytes 263168 | tf_op jit(solution)/shard_map/neg | solution.py:30
  77.0 4.7 %all-to-all-done.3 = bf16[8,32,512]{2,1,0:T(8,128)(2,1)S(1)} async-done(((bf16[8,32,512]{2,1,0:T(8,128)(2,1)}), bf16[8,32,512]{2,1,0:T(8,128)(2,1)S(1)}, u32[]{:S(2)}, u32[]{:S(2)}) %all-to-all-start.3) | async-done | bytes 262176 | tf_op jit(solution)/shard_map/all_to_all | solution.py:167
  81.6 1.8 %convolution_multiply_fusion.1 = f32[512,1024]{1,0:T(8,128)S(1)} fusion(bf16[256,512]{1,0:T(8,128)(2,1)S(1)} %bitcast.220, bf16[256,512]{1,0:T(8,128)(2,1)} %bitcast.20, bf16[256,512]{1,0:T(8,128)(2,1)S(1)} %copy-done.8, bf16[256,512]{1,0:T(8,128)(2,1)S(1)} %get-tuple-element.25, bf16[256,512]{1,0:T(8,128)(2,1)S(1)} %fusion.98), kind=kOutput, calls=%fused_computation.9 | convolution fusion | flops 542638080 | bytes 3407872 | tf_op jit(solution)/shard_map/jr,jo->ro/dot_general | solution.py:191
  86.0 9.3 %all_to_all.106 = bf16[8,32,512]{2,1,0:T(8,128)(2,1)S(1)} all-to-all(bf16[8,32,512]{2,1,0:T(8,128)(2,1)S(1)} %bitcast.217), channel_id=1, replica_groups=mesh['trial'=4,'row'=8] {'row'}, dimensions={0} | all-to-all | bytes 524288 | tf_op jit(solution)/shard_map/all_to_all | solution.py:118
  95.3 3.6 %all-to-all-start.5 = ((bf16[8,32,512]{2,1,0:T(8,128)(2,1)}), bf16[8,32,512]{2,1,0:T(8,128)(2,1)S(1)}, u32[]{:S(2)}, u32[]{:S(2)}) async-start(bf16[8,32,512]{2,1,0:T(8,128)(2,1)} %bitcast.34), calls=%async_computation.5 | async-start | bytes 524288 | tf_op jit(solution)/shard_map/all_to_all | solution.py:119
  99.5 6.1 %all-to-all-done.5 = bf16[8,32,512]{2,1,0:T(8,128)(2,1)S(1)} async-done(((bf16[8,32,512]{2,1,0:T(8,128)(2,1)}), bf16[8,32,512]{2,1,0:T(8,128)(2,1)S(1)}, u32[]{:S(2)}, u32[]{:S(2)}) %all-to-all-start.5) | async-done | bytes 262176 | tf_op jit(solution)/shard_map/all_to_all | solution.py:119
  108.1 2.4 %subtract_convert_fusion.1 = (bf16[32,8,512]{2,1,0:T(8,128)(2,1)S(1)}, bf16[32,8,512]{2,1,0:T(8,128)(2,1)S(1)}) fusion(f32[32,8,1024]{2,1,0:T(8,128)S(1)} %fusion.8, f32[32]{0:T(128)S(1)} %multiply_multiply_fusion, f32[8,512]{1,0:T(8,128)S(1)} %fusion.106, f32[]{:T(128)} %bitcast.14), kind=kLoop, calls=%fused_computation.104 | loop fusion | flops 1441792 | bytes 1589380 | tf_op jit(solution)/shard_map/convert_element_type | solution.py:188
  113.4 4.0 %all-to-all-start.6 = ((bf16[32,8,512]{2,0,1:T(8,128)(2,1)}), bf16[32,8,512]{2,0,1:T(8,128)(2,1)}, u32[]{:S(2)}, u32[]{:S(2)}) async-start(bf16[32,8,512]{2,0,1:T(8,128)(2,1)} %copy.61), calls=%async_computation.6 | async-start | bytes 524288 | tf_op jit(solution)/shard_map/all_to_all | solution.py:165
  118.1 6.2 %all-to-all-done.6 = bf16[32,8,512]{2,0,1:T(8,128)(2,1)} async-done(((bf16[32,8,512]{2,0,1:T(8,128)(2,1)}), bf16[32,8,512]{2,0,1:T(8,128)(2,1)}, u32[]{:S(2)}, u32[]{:S(2)}) %all-to-all-start.6) | async-done | bytes 262176 | tf_op jit(solution)/shard_map/all_to_all | solution.py:165
  124.4 9.3 %all_to_all.107 = bf16[8,32,512]{2,1,0:T(8,128)(2,1)S(1)} all-to-all(bf16[8,32,512]{2,1,0:T(8,128)(2,1)S(1)} %constant_dynamic-update-slice_fusion.8), channel_id=1, replica_groups=mesh['trial'=4,'row'=8] {'row'}, dimensions={0} | all-to-all | bytes 524288 | tf_op jit(solution)/shard_map/all_to_all | solution.py:167
  133.7 1.8 %convolution_multiply_fusion = f32[512,1024]{1,0:T(8,128)S(1)} fusion(bf16[256,512]{1,0:T(8,128)(2,1)S(1)} %bitcast.221, bf16[256,512]{1,0:T(8,128)(2,1)} %bitcast.43, bf16[256,512]{1,0:T(8,128)(2,1)S(1)} %copy-done.9, bf16[256,512]{1,0:T(8,128)(2,1)S(1)} %get-tuple-element.25, bf16[256,512]{1,0:T(8,128)(2,1)} %copy-done.16), kind=kOutput, calls=%fused_computation.8 | convolution fusion | flops 542638080 | bytes 3407872 | tf_op jit(solution)/shard_map/jr,jo->ro/dot_general | solution.py:191
  135.5 4.3 %fusion.31 = bf16[512,512]{1,0:T(8,128)(2,1)S(1)} fusion(f32[512,1024]{1,0:T(8,128)S(1)} %convolution_multiply_fusion, s32[512]{0:T(512)S(1)} %get-tuple-element.29, s32[512]{0:T(512)S(1)} %get-tuple-element.30, s32[512]{0:T(512)S(1)} %add_select_fusion.6, f32[512,512]{1,0:T(8,128)S(1)} %copy-done, f32[64,8,4,128]{3,2,1,0:T(4,128)S(1)} %bitcast.199), kind=kLoop, calls=%fused_computation.48 | loop fusion | flops 2883584 | bytes 4724736 | tf_op jit(solution)/shard_map/convert_element_type | solution.py:211
  139.8 1.0 copy.78
  140.8 21.4 %reduce-scatter.4.cloned.1.call-done = bf16[128,512]{1,0:T(8,128)(2,1)} async-done(((bf16[512,512]{1,0:T(8,128)(2,1)}), bf16[128,512]{1,0:T(8,128)(2,1)}) %reduce-scatter.4.cloned.1.call-update) | async-done | bytes 131088
  162.2 1.0 copy.79
  (91 shorter events, 22.2 us)
Async XLA Ops:
  6.5 6.2 %copy-start = (f32[512,512]{1,0:T(8,128)S(1)}, f32[512,512]{1,0:T(8,128)}, u32[]{:S(2)}) copy-start(f32[512,512]{1,0:T(8,128)} %param.7) | copy-start | bytes 3145732
  8.6 8.4 %copy-start.10 = (bf16[512,256]{1,0:T(8,128)(2,1)}, bf16[512,256]{1,0:T(8,128)(2,1)S(1)}, u32[]{:S(2)}) copy-start(bf16[512,256]{1,0:T(8,128)(2,1)S(1)} %fusion.97) | copy-start | bytes 786436
  10.8 6.2 %copy-start.12 = (bf16[512,256]{1,0:T(8,128)(2,1)}, bf16[512,256]{1,0:T(8,128)(2,1)S(1)}, u32[]{:S(2)}) copy-start(bf16[512,256]{1,0:T(8,128)(2,1)S(1)} %get-tuple-element.27) | copy-start | bytes 786436
  10.8 6.2 %copy-start.14 = (bf16[512,256]{1,0:T(8,128)(2,1)}, bf16[512,256]{1,0:T(8,128)(2,1)S(1)}, u32[]{:S(2)}) copy-start(bf16[512,256]{1,0:T(8,128)(2,1)S(1)} %get-tuple-element.28) | copy-start | bytes 786436
  18.6 22.9 %all-to-all-start = ((bf16[8,32,512]{2,1,0:T(8,128)(2,1)}), bf16[8,32,512]{2,1,0:T(8,128)(2,1)S(1)}, u32[]{:S(2)}, u32[]{:S(2)}) async-start(bf16[8,32,512]{2,1,0:T(8,128)(2,1)} %bitcast.3), calls=%async_computation | async-start | bytes 524288 | tf_op jit(solution)/shard_map/all_to_all | solution.py:118
  41.5 11.1 %all-to-all-start.1 = ((bf16[8,32,512]{2,1,0:T(8,128)(2,1)}), bf16[8,32,512]{2,1,0:T(8,128)(2,1)S(1)}, u32[]{:S(2)}, u32[]{:S(2)}) async-start(bf16[8,32,512]{2,1,0:T(8,128)(2,1)} %bitcast.6), calls=%async_computation.1 | async-start | bytes 524288 | tf_op jit(solution)/shard_map/all_to_all | solution.py:119
  52.6 1.7 copy-start.2
  52.6 1.7 copy-start.4
  52.6 1.7 copy-start.6
  59.6 22.0 %copy-start.8 = (bf16[256,512]{1,0:T(8,128)(2,1)S(1)}, bf16[256,512]{1,0:T(8,128)(2,1)}, u32[]{:S(2)}) copy-start(bf16[256,512]{1,0:T(8,128)(2,1)} %get-tuple-element.26) | copy-start | bytes 786436
  60.4 11.0 %all-to-all-start.2 = ((bf16[32,8,512]{2,0,1:T(8,128)(2,1)}), bf16[32,8,512]{2,0,1:T(8,128)(2,1)}, u32[]{:S(2)}, u32[]{:S(2)}) async-start(bf16[32,8,512]{2,0,1:T(8,128)(2,1)} %copy.54), calls=%async_computation.2 | async-start | bytes 524288 | tf_op jit(solution)/shard_map/all_to_all | solution.py:165
  71.4 10.3 %all-to-all-start.3 = ((bf16[8,32,512]{2,1,0:T(8,128)(2,1)}), bf16[8,32,512]{2,1,0:T(8,128)(2,1)S(1)}, u32[]{:S(2)}, u32[]{:S(2)}) async-start(bf16[8,32,512]{2,1,0:T(8,128)(2,1)} %constant_dynamic-update-slice_fusion), calls=%async_computation.3 | async-start | bytes 524288 | tf_op jit(solution)/shard_map/all_to_all | solution.py:167
  76.9 8.3 %copy-start.16 = (bf16[256,512]{1,0:T(8,128)(2,1)}, bf16[256,512]{1,0:T(8,128)(2,1)S(1)}, u32[]{:S(2)}) copy-start(bf16[256,512]{1,0:T(8,128)(2,1)S(1)} %fusion.98) | copy-start | bytes 786436
  81.6 1.8 %copy-start.1 = (f32[512,512]{1,0:T(8,128)S(1)}, f32[512,512]{1,0:T(8,128)}, u32[]{:S(2)}) copy-start(f32[512,512]{1,0:T(8,128)} %param.8) | copy-start | bytes 3145732
  83.4 1.0 copy-start.11
  83.4 1.0 copy-start.13
  83.4 1.1 copy-start.15
  95.3 10.3 %all-to-all-start.5 = ((bf16[8,32,512]{2,1,0:T(8,128)(2,1)}), bf16[8,32,512]{2,1,0:T(8,128)(2,1)S(1)}, u32[]{:S(2)}, u32[]{:S(2)}) async-start(bf16[8,32,512]{2,1,0:T(8,128)(2,1)} %bitcast.34), calls=%async_computation.5 | async-start | bytes 524288 | tf_op jit(solution)/shard_map/all_to_all | solution.py:119
  105.6 1.7 copy-start.3
  105.6 1.7 copy-start.5
  105.6 1.7 copy-start.7
  112.6 21.1 %copy-start.9 = (bf16[256,512]{1,0:T(8,128)(2,1)S(1)}, bf16[256,512]{1,0:T(8,128)(2,1)}, u32[]{:S(2)}) copy-start(bf16[256,512]{1,0:T(8,128)(2,1)} %get-tuple-element.26) | copy-start | bytes 786436
  113.4 11.0 %all-to-all-start.6 = ((bf16[32,8,512]{2,0,1:T(8,128)(2,1)}), bf16[32,8,512]{2,0,1:T(8,128)(2,1)}, u32[]{:S(2)}, u32[]{:S(2)}) async-start(bf16[32,8,512]{2,0,1:T(8,128)(2,1)} %copy.61), calls=%async_computation.6 | async-start | bytes 524288 | tf_op jit(solution)/shard_map/all_to_all | solution.py:165
  117.5 44.7 %reduce-scatter.4.cloned.1.call-start = ((), (), s32[]{:S(2)}) async-start(), calls=%async_computation.9 | async-start | bytes 655360
Sparse Core Ops, SparseCore 0:
  141.0 21.1 reduce-scatter.3
